TPU v7x, 128 devices: a whole 4x4x4 slice. The times are simulated.
128 devices in a mesh: row: 8 (over z, x_hi), col: 16 (over x_lo, y, core).
Axes of the slice: x: 4 (x_hi: 2, x_lo: 2; x = x_hi * 2 + x_lo), y: 4, z: 4, core: 2. Of those that a mesh axis runs over, the one named last changes fastest.
Arguments:
- ingest_features: bfloat16 [32768, 1536], P(('row', 'col')), may hold values from -40 to 40
- node_map: int32 [32768], P(('row', 'col')), may hold values from 0 to 16383, as said below
- unit_rows: int32 [128], P(('row', 'col')), may hold values from 0 to 256, as said below
- tile_ids: int32 [12288, 2], P(('row', 'col')), may hold values from 0 to 128, as said below
- tile_values: bfloat16 [12288, 128, 128], P(('row', 'col')), may hold values from -40 to 40
- mix_in: bfloat16 [128, 128], replicated, may hold values from -0.5 to 0.5
- mix_out: bfloat16 [128, 128], replicated, may hold values from -0.5 to 0.5
Outputs:
- residual: float32 [16384, 1536], P(('row', 'col'))
Inputs may be any that keep to these rules, and one draw needn't show every extreme that they name: `node_map`: for every unit u the first unit_rows[u] of its 256 slots name distinct nodes, and all units' such slots together name every node exactly once; at most 2 of them of one unit name nodes of one partition (nodes k * 128 to (k + 1) * 128 - 1), and one unit names exactly 2 in every partition. Entries of the other slots are arbitrary nodes. `unit_rows`: one unit delivers 256 rows. `tile_ids`: slots k * 96 to (k + 1) * 96 - 1 hold first some distinct tiles whose row tile lies in row block k // 16 (tile rows (16 times that) onward) and whose column tile lies in column block k % 16, then padding slots whose row tile and column tile are both 16384 // 128. Some blocks have no padding slot.
All inputs are finite; a program needn't handle non-finite values.
Results may differ from a plain program's by a relative error of at most 0.0095.
Values may be sent and summed in bfloat16 or wider, within the bound.
A program may use at most 64 MiB of HBM per device.

v0:
```python
import jax
import jax.numpy as jnp
from jax import lax
from jax.sharding import PartitionSpec as P

CH = 128
TILE = 128
PIECE = 128


epsilon = 1e-05


def normalize(values):
    groups = values.reshape(-1, CH)
    power = jnp.mean(groups * groups, axis=-1, keepdims=True)
    return (groups * lax.rsqrt(power + epsilon)).astype(jnp.bfloat16)


def encode(totals, mix_in):
    row_total = totals.shape[0]
    mixed = jnp.dot(normalize(totals), mix_in, preferred_element_type=jnp.float32)
    return jax.nn.gelu(mixed, approximate=False).astype(jnp.bfloat16).reshape(row_total, -1)


def dense_block(tile_ids, tile_values, row_index, col_index, row_tiles, col_tiles):
    local_rows = tile_ids[:, 0] - row_index * row_tiles
    local_cols = tile_ids[:, 1] - col_index * col_tiles
    tile_edge = tile_values.shape[1]
    tile_grid = jnp.zeros((row_tiles, col_tiles, tile_edge, tile_edge), tile_values.dtype)
    tile_grid = tile_grid.at[local_rows, local_cols].set(tile_values, mode="drop")
    return tile_grid.transpose(0, 2, 1, 3).reshape(row_tiles * tile_edge, col_tiles * tile_edge)


def local(ingest_features, node_map, unit_rows, tile_ids, tile_values, mix_in, mix_out):
    row_count = lax.axis_size("row")
    col_count = lax.axis_size("col")
    unit_count = row_count * col_count
    slots_held = node_map.shape[0]
    per_pair = slots_held // unit_count
    feature_width = ingest_features.shape[1]
    owner = node_map // PIECE
    live = jnp.arange(slots_held, dtype=jnp.int32) < unit_rows[0]
    member = (
        (owner[:, None] == jnp.arange(unit_count, dtype=jnp.int32)[None, :]) & live[:, None]
    ).astype(jnp.int32)
    earlier = jnp.cumsum(member, axis=0) - member
    rank_within = jnp.sum(earlier * member, axis=1)
    target = jnp.where(live, owner * per_pair + rank_within, unit_count * per_pair)
    outgoing = (
        jnp.zeros((unit_count * per_pair, feature_width), jnp.bfloat16)
        .at[target]
        .set(ingest_features, mode="drop")
    )
    placing = (
        jnp.full((unit_count * per_pair,), -1, jnp.int32)
        .at[target]
        .set(node_map % PIECE, mode="drop")
    )
    arrived, arrived_at = (
        lax.all_to_all(
            outgoing.reshape(unit_count, per_pair, feature_width),
            ("row", "col"),
            split_axis=0,
            concat_axis=0,
            tiled=True,
        ),
        lax.all_to_all(
            placing.reshape(unit_count, per_pair),
            ("row", "col"),
            split_axis=0,
            concat_axis=0,
            tiled=True,
        ),
    )
    arrived = arrived.reshape(-1, feature_width)
    arrived_at = arrived_at.reshape(-1)
    landing = jnp.where(arrived_at >= 0, arrived_at, PIECE)
    features = jnp.zeros((PIECE, feature_width), jnp.bfloat16).at[landing].set(arrived, mode="drop")
    row_tiles = col_count * PIECE // TILE
    col_tiles = row_count * PIECE // TILE
    block = dense_block(
        tile_ids, tile_values, lax.axis_index("row"), lax.axis_index("col"), row_tiles, col_tiles
    )
    strip = block
    back_part = lax.dot_general(
        strip,
        lax.all_gather(features, "col", axis=0, tiled=True),
        (((0,), (0,)), ((), ())),
        preferred_element_type=jnp.float32,
    )
    back_own = lax.psum_scatter(
        back_part.astype(jnp.bfloat16), "row", scatter_dimension=0, tiled=True
    ).astype(jnp.float32)
    hidden = lax.all_gather(encode(back_own, mix_in), "row", axis=0, tiled=True)
    strip = block
    forward_sum = lax.psum_scatter(
        jnp.dot(strip, hidden, preferred_element_type=jnp.float32).astype(jnp.bfloat16),
        "col",
        scatter_dimension=0,
        tiled=True,
    ).astype(jnp.float32)
    recon = jnp.dot(normalize(forward_sum), mix_out, preferred_element_type=jnp.float32).reshape(
        PIECE, feature_width
    )
    return features.astype(jnp.float32) - recon


def solution(mesh):
    return jax.shard_map(
        local,
        mesh=mesh,
        in_specs=(
            P(("row", "col"), None),
            P(("row", "col")),
            P(("row", "col")),
            P(("row", "col"), None),
            P(("row", "col"), None, None),
            P(),
            P(),
        ),
        out_specs=P(("row", "col"), None),
        check_vma=False,
    )
```

profile of v0, /device:TPU:0, one launch (start us, length us, event | category | flops | bytes accessed | tf_op | source)
XLA Modules:
  0.0 343.9 jit_solution(6542489902503923748)
XLA Ops:
  6.5 0.0 copy-start
  7.2 0.7 and_select_fusion
  7.9 0.1 copy.11
  8.1 0.3 fusion.26
  8.5 0.2 fusion.28
  8.7 1.4 scatter_custom_fusion
  10.1 0.8 all_to_all.9
  10.9 11.1 %all-to-all-start = ((s32[128,1,2]{2,1,0:T(1,128)}), s32[128,1,2]{2,1,0:T(1,128)S(1)}, u32[]{:S(2)}, u32[]{:S(2)}) async-start(s32[128,1,2]{2,1,0:T(1,128)} %bitcast.5), calls=%async_computation | async-start | bytes 131072 | tf_op jit(solution)/shard_map/all_to_all | solution.py:68
  22.0 2.6 scatter_custom_fusion.1
  24.6 1.2 reshape.107
  25.8 5.5 %all-to-all-done = s32[128,1,2]{2,1,0:T(1,128)S(1)} async-done(((s32[128,1,2]{2,1,0:T(1,128)}), s32[128,1,2]{2,1,0:T(1,128)S(1)}, u32[]{:S(2)}, u32[]{:S(2)}) %all-to-all-start) | async-done | bytes 1056 | tf_op jit(solution)/shard_map/all_to_all | solution.py:68
  31.3 4.7 %all-to-all-start.1 = ((bf16[128,2,1536]{2,1,0:T(2,128)(2,1)}), bf16[128,2,1536]{2,1,0:T(2,128)(2,1)S(1)}, u32[]{:S(2)}, u32[]{:S(2)}) async-start(bf16[128,2,1536]{2,1,0:T(2,128)(2,1)} %reshape.107), calls=%async_computation.1 | async-start | bytes 1572864 | tf_op jit(solution)/shard_map/all_to_all | solution.py:61
  36.0 0.0 all-gather.3.cloned.1.call-start
  36.1 0.6 broadcast.166
  36.7 0.8 reduce.3
  37.5 0.1 reshape.106
  37.7 14.6 %all-to-all-done.1 = bf16[128,2,1536]{2,1,0:T(2,128)(2,1)S(1)} async-done(((bf16[128,2,1536]{2,1,0:T(2,128)(2,1)}), bf16[128,2,1536]{2,1,0:T(2,128)(2,1)S(1)}, u32[]{:S(2)}, u32[]{:S(2)}) %all-to-all-start.1) | async-done | bytes 786464 | tf_op jit(solution)/shard_map/all_to_all | solution.py:61
  52.3 1.2 reshape.140
  53.5 3.2 scatter_custom_fusion.2
  56.7 0.0 all-gather.3.cloned.1.call-update
  56.8 0.2 reduce-scatter.3.cloned.1.call-start
  57.0 0.0 copy-done.4
  57.0 3.1 broadcast_in_dim.34
  60.2 0.0 copy-done.2
  60.2 13.7 %scatter_fusion = bf16[16,8,128,128]{3,2,1,0:T(8,128)(2,1)} fusion(bf16[16,8,128,128]{3,2,1,0:T(8,128)(2,1)} %broadcast_in_dim.34, s32[96]{0:T(128)S(1)} %fusion.36, bf16[96,128,128]{2,1,0:T(8,128)(2,1)S(1)} %copy-done.2), kind=kCustom, calls=%fused_computation.3 | custom fusion | bytes 9437952 | tf_op jit(solution)/shard_map/scatter | solution.py:31
  73.9 7.9 %copy.14 = bf16[16,128,8,128]{3,2,1,0:T(8,128)(2,1)} copy(bf16[16,128,8,128]{3,1,2,0:T(8,128)(2,1)} %bitcast.40) | data formatting | bytes 8388608 | tf_op jit(solution)/shard_map/transpose | solution.py:32
  81.8 13.2 %all-gather.3.cloned.1.call-done = bf16[2048,1536]{1,0:T(8,128)(2,1)} async-done(((bf16[128,1536]{1,0:T(8,128)(2,1)}), bf16[2048,1536]{1,0:T(8,128)(2,1)}) %all-gather.3.cloned.1.call-update) | async-done | bytes 6291472 | tf_op jit(solution)/shard_map/all_gather | solution.py:88
  95.0 11.4 %fusion.3 = bf16[1024,1536]{1,0:T(8,128)(2,1)} fusion(bf16[2048,1536]{1,0:T(8,128)(2,1)} %all-gather.3.cloned.1.call-done, bf16[256,8,8,128]{3,2,1,0:T(8,128)(2,1)} %bitcast.41), kind=kOutput, calls=%fused_computation.8 | convolution fusion | flops 6444023808 | bytes 13631488 | tf_op jit(solution)/shard_map/dot_general | solution.py:86
  106.4 0.0 reduce-scatter.3.cloned.1.call-update
  106.5 0.0 all-gather.5.cloned.1.call-start
  106.5 80.5 %reduce-scatter.3.cloned.1.call-done = bf16[128,1536]{1,0:T(8,128)(2,1)} async-done(((bf16[1024,1536]{1,0:T(8,128)(2,1)}), bf16[128,1536]{1,0:T(8,128)(2,1)}) %reduce-scatter.3.cloned.1.call-update) | async-done | bytes 393232 | tf_op jit(solution)/shard_map/reduce_scatter | solution.py:92
  187.0 1.4 reshape.117
  188.4 0.3 multiply_reduce_fusion.1
  188.7 0.0 copy-done
  188.7 2.4 fusion.10
  191.1 1.2 reshape.112
  192.3 0.0 all-gather.5.cloned.1.call-update
  192.3 0.3 reduce-scatter.5.cloned.1.call-start
  192.6 61.5 %all-gather.5.cloned.1.call-done = bf16[1024,1536]{1,0:T(8,128)(2,1)} async-done(((bf16[128,1536]{1,0:T(8,128)(2,1)}), bf16[1024,1536]{1,0:T(8,128)(2,1)}) %all-gather.5.cloned.1.call-update) | async-done | bytes 3145744 | tf_op jit(solution)/shard_map/all_gather | solution.py:95
  254.2 11.3 %convolution_convert_fusion = bf16[2048,1536]{1,0:T(8,128)(2,1)} fusion(bf16[1024,1536]{1,0:T(8,128)(2,1)} %all-gather.5.cloned.1.call-done, bf16[256,8,8,128]{3,2,1,0:T(8,128)(2,1)} %bitcast.42), kind=kOutput, calls=%fused_computation.4 | convolution fusion | flops 6445596672 | bytes 13631488 | tf_op jit(solution)/shard_map/dot_general | solution.py:98
  265.5 0.0 reduce-scatter.5.cloned.1.call-update
  265.5 68.6 %reduce-scatter.5.cloned.1.call-done = bf16[128,1536]{1,0:T(8,128)(2,1)} async-done(((bf16[2048,1536]{1,0:T(8,128)(2,1)}), bf16[128,1536]{1,0:T(8,128)(2,1)}) %reduce-scatter.5.cloned.1.call-update) | async-done | bytes 393232 | tf_op jit(solution)/shard_map/reduce_scatter | solution.py:97
  334.1 1.4 reshape.119
  335.6 0.3 multiply_reduce_fusion
  335.9 0.4 fusion.19
  336.3 0.1 reshape.115
  336.4 0.0 copy-done.1
  336.4 1.0 convert_subtract_fusion
  (18 shorter events, 0.1 us)
Async XLA Ops:
  6.5 182.2 %copy-start = (bf16[128,128]{1,0:T(8,128)(2,1)S(1)}, bf16[128,128]{1,0:T(8,128)(2,1)}, u32[]{:S(2)}) copy-start(bf16[128,128]{1,0:T(8,128)(2,1)} %param.12) | copy-start | bytes 98308
  6.5 50.5 %copy-start.4 = (s32[96,2]{0,1:T(2,128)S(1)}, s32[96,2]{0,1:T(2,128)}, u32[]{:S(2)}) copy-start(s32[96,2]{0,1:T(2,128)} %param.10) | copy-start | bytes 2308
  10.9 20.5 %all-to-all-start = ((s32[128,1,2]{2,1,0:T(1,128)}), s32[128,1,2]{2,1,0:T(1,128)S(1)}, u32[]{:S(2)}, u32[]{:S(2)}) async-start(s32[128,1,2]{2,1,0:T(1,128)} %bitcast.5), calls=%async_computation | async-start | bytes 131072 | tf_op jit(solution)/shard_map/all_to_all | solution.py:68
  31.3 21.0 %all-to-all-start.1 = ((bf16[128,2,1536]{2,1,0:T(2,128)(2,1)}), bf16[128,2,1536]{2,1,0:T(2,128)(2,1)S(1)}, u32[]{:S(2)}, u32[]{:S(2)}) async-start(bf16[128,2,1536]{2,1,0:T(2,128)(2,1)} %reshape.107), calls=%async_computation.1 | async-start | bytes 1572864 | tf_op jit(solution)/shard_map/all_to_all | solution.py:61
  36.0 59.0 %all-gather.3.cloned.1.call-start = ((), (), s32[]{:S(2)}) async-start(), calls=%async_computation.4 | async-start | bytes 6684672 | tf_op jit(solution)/shard_map/all_gather | solution.py:88
  53.5 6.7 %copy-start.2 = (bf16[96,128,128]{2,1,0:T(8,128)(2,1)S(1)}, bf16[96,128,128]{2,1,0:T(8,128)(2,1)}, u32[]{:S(2)}) copy-start(bf16[96,128,128]{2,1,0:T(8,128)(2,1)} %param.11) | copy-start | bytes 9437188
  56.8 130.2 %reduce-scatter.3.cloned.1.call-start = ((), (), s32[]{:S(2)}) async-start(), calls=%async_computation.5 | async-start | bytes 3538944 | tf_op jit(solution)/shard_map/reduce_scatter | solution.py:92
  106.5 147.7 %all-gather.5.cloned.1.call-start = ((), (), s32[]{:S(2)}) async-start(), calls=%async_computation.6 | async-start | bytes 3538944 | tf_op jit(solution)/shard_map/all_gather | solution.py:95
  192.3 141.8 %reduce-scatter.5.cloned.1.call-start = ((), (), s32[]{:S(2)}) async-start(), calls=%async_computation.7 | async-start | bytes 6684672 | tf_op jit(solution)/shard_map/reduce_scatter | solution.py:97
  265.5 70.4 %copy-start.3 = (bf16[128,128]{1,0:T(8,128)(2,1)S(1)}, bf16[128,128]{1,0:T(8,128)(2,1)}, u32[]{:S(2)}) copy-start(bf16[128,128]{1,0:T(8,128)(2,1)} %param.13) | copy-start | bytes 98308
  265.5 70.9 %copy-start.1 = (bf16[128,1536]{1,0:T(8,128)(2,1)S(1)}, bf16[128,1536]{1,0:T(8,128)(2,1)}, u32[]{:S(2)}) copy-start(bf16[128,1536]{1,0:T(8,128)(2,1)} %scatter_custom_fusion.2) | copy-start | bytes 1179652
Sparse Core Ops, SparseCore 0:
  56.9 38.0 all-gather.2
  106.6 80.3 reduce-scatter.2
  192.5 61.6 all-gather.4
  265.6 68.4 reduce-scatter.4
where the time goes:
time: 345 us; the launch traced here: 344 us
  waiting for transfers between devices  244 us (71%)
  local copies, waits for them, and re-layouts  40.2 us (12%)
  matrix products  25.5 us (7%)
  starting transfers between devices  16.4 us (5%)
  between operations  14 us (4%)
  other arithmetic  3.71 us (1%)
    reduce_scatter x1, waiting for transfers between devices, local(): lax.psum_scatter(back_part.astype(jnp.bfloat16), 'row', scatter_dimension...  80.5 us
    reduce_scatter x1, waiting for transfers between devices, local(): lax.psum_scatter(jnp.dot(strip, hidden, preferred_element_type=jnp.float3...  68.6 us
    all_gather x1, waiting for transfers between devices, local(): hidden = lax.all_gather(encode(back_own, mix_in), 'row', axis=0, tiled=True)  61.5 us
    all_to_all x1, waiting for transfers between devices, local(): lax.all_to_all(outgoing.reshape(unit_count, per_pair, feature_width), ('r...  14.6 us
    scatter x1, local copies, waits for them, and re-layouts, dense_block(): tile_grid.at[local_rows, local_cols].set(tile_values, mode='drop')  13.7 us
    all_gather x1, waiting for transfers between devices, local(): lax.all_gather(features, 'col', axis=0, tiled=True)  13.2 us
    dot_general x1, matrix products, local(): lax.dot_general(strip, lax.all_gather(features, 'col', axis=0, tiled=True...  11.4 us
    dot_general x1, matrix products, local(): jnp.dot(strip, hidden, preferred_element_type=jnp.float32)  11.3 us
  transfers between devices with their start and end apart: 6, of which 6 were waited for; matrix products, arithmetic and copies ran while one was open for 9% of the time, Pallas kernels for 0%

commit v1 on v0

v1 whole, which is shorter than its diff:
```python
import functools

import jax
import jax.numpy as jnp
from jax import lax
from jax.experimental import pallas as pl
from jax.experimental.pallas import tpu as pltpu
from jax.sharding import PartitionSpec as P

CH = 128
TILE = 128
PIECE = 128
CHUNKS = 3
LAG = 3
MESH = pl.DeviceIdType.MESH

epsilon = 1e-05


def normalize(groups):
    power = jnp.mean(groups * groups, axis=-1, keepdims=True)
    return (groups * lax.rsqrt(power + epsilon)).astype(jnp.bfloat16)


def gelu(v):
    return 0.5 * v * (1.0 + lax.erf(v * (0.5**0.5)))


class Ring:
    def __init__(self, place, bit, forward, backward, mate):
        self.place, self.bit = place, bit
        self.forward, self.backward, self.mate = forward, backward, mate

    def slot(self, step, other):
        bit = 1 - self.bit if other else self.bit
        return lax.rem(self.place + step + 4, 4) * 2 + bit


def block_kernel(slot_ref, tiles_ref, block_ref, flipped_ref):
    place = pl.program_id(0)
    for col in range(block_ref.shape[1] // TILE):
        slot = slot_ref[place * (block_ref.shape[1] // TILE) + col]
        tile = tiles_ref[jnp.maximum(slot, 0)]
        tile = jnp.where(slot >= 0, tile, jnp.zeros_like(tile))
        block_ref[:, col * TILE : (col + 1) * TILE] = tile
        flipped_ref[col * TILE : (col + 1) * TILE, :] = tile.T


def build_block(slot_of, tile_values, row_tiles, col_tiles):
    rows, cols = row_tiles * TILE, col_tiles * TILE
    return pl.pallas_call(
        block_kernel,
        grid_spec=pltpu.PrefetchScalarGridSpec(
            num_scalar_prefetch=1,
            grid=(row_tiles,),
            in_specs=[pl.BlockSpec(tile_values.shape, lambda i, s: (0, 0, 0))],
            out_specs=[
                pl.BlockSpec((TILE, cols), lambda i, s: (i, 0)),
                pl.BlockSpec((cols, TILE), lambda i, s: (0, i)),
            ],
        ),
        out_shape=[
            jax.ShapeDtypeStruct((rows, cols), jnp.bfloat16),
            jax.ShapeDtypeStruct((cols, rows), jnp.bfloat16),
        ],
        cost_estimate=pl.CostEstimate(flops=0, bytes_accessed=24 << 20, transcendentals=0),
        name="build_block",
    )(slot_of, tile_values)


def hops_kernel(
    features_ref, block_hbm, flipped_hbm, mix_in_ref, mix_out_ref, out_ref,
    block, flipped, panel, back, hidden, ahead, across,
    row_near, row_pair, row_sum, row_mate, col_near, col_pair, col_sum, col_mate,
    local_sem, panel_send, panel_recv, core_send, core_recv, hidden_send, hidden_recv,
    row_send, row_recv, col_send, col_recv, swap_send, swap_recv,
):
    width = panel.shape[-1]
    r, q = lax.axis_index("row"), lax.axis_index("col")
    core, y, xl = lax.rem(q, 2), lax.rem(q // 2, 4), q // 8
    z, xh = r // 2, lax.rem(r, 2)

    def col_of(xl_, y_, core_):
        return {"col": (xl_ * 4 + y_) * 2 + core_}

    def row_of(z_, xh_):
        return {"row": z_ * 2 + xh_}

    partner = col_of(xl, y, 1 - core)
    col_ring = Ring(
        y, xl, col_of(xl, lax.rem(y + 1, 4), core), col_of(xl, lax.rem(y + 3, 4), core), col_of(1 - xl, y, core)
    )
    row_ring = Ring(
        z, xh, row_of(lax.rem(z + 1, 4), xh), row_of(lax.rem(z + 3, 4), xh), row_of(z, 1 - xh)
    )

    block_copy = pltpu.make_async_copy(block_hbm, block, local_sem.at[0])
    flipped_copy = pltpu.make_async_copy(flipped_hbm, flipped, local_sem.at[1])
    flipped_copy.start()
    block_copy.start()

    barrier = pltpu.get_barrier_semaphore()
    neighbours = [partner] + [d for g in (col_ring, row_ring) for d in (g.forward, g.backward, g.mate)]
    for device in neighbours:
        pl.semaphore_signal(barrier, inc=1, device_id=device, device_id_type=MESH)
    pl.semaphore_wait(barrier, len(neighbours))

    sent = []

    def send(src, dst, send_sem, recv_sem, device):
        copy = pltpu.make_async_remote_copy(
            src_ref=src, dst_ref=dst, send_sem=send_sem, recv_sem=recv_sem, device_id=device, device_id_type=MESH
        )
        copy.start()
        sent.append(copy)

    def await_recv(dst, send_sem, recv_sem, device):
        pltpu.make_async_remote_copy(
            src_ref=dst, dst_ref=dst, send_sem=send_sem, recv_sem=recv_sem, device_id=device, device_id_type=MESH
        ).wait_recv()

    class Gather:
        def __init__(self, c, ring, buf, base, send_sem, recv_sem):
            self.c, self.ring, self.buf, self.base = c, ring, buf, base
            self.ss, self.rs = send_sem, recv_sem
            self.slots = [
                ring.slot(0, True), ring.slot(-1, False), ring.slot(1, False), ring.slot(-1, True),
                ring.slot(1, True), ring.slot(2, False), ring.slot(2, True),
            ]

        def at(self, slot):
            return self.buf.at[self.c, self.base + slot]

        def push(self, src, slot, kind, device):
            send(src, self.at(slot), self.ss.at[self.c, kind], self.rs.at[self.c, kind], device)

        def wait(self, kind):
            await_recv(self.at(self.slots[kind]), self.ss.at[self.c, kind], self.rs.at[self.c, kind], self.ring.mate)

        def first(self, src):
            own = self.ring.slot(0, False)
            self.push(src, own, 0, self.ring.mate)
            self.push(src, own, 1, self.ring.forward)
            self.push(src, own, 2, self.ring.backward)

        def second(self):
            self.wait(0)
            slot = self.slots[0]
            self.push(self.at(slot), slot, 3, self.ring.forward)
            self.push(self.at(slot), slot, 4, self.ring.backward)

        def third(self, also=None):
            self.wait(1)
            self.push(self.at(self.slots[1]), self.slots[1], 5, self.ring.forward)
            self.wait(2)
            self.wait(4)
            self.push(self.at(self.slots[4]), self.slots[4], 6, self.ring.backward)
            self.wait(3)

        def fourth(self):
            self.wait(5)
            self.wait(6)

    class Scatter:
        def __init__(self, c, ring, buf, base, near, pair, total, mate, send_sem, recv_sem):
            self.c, self.ring, self.buf, self.base = c, ring, buf, base
            self.near, self.pair, self.total, self.mate = near, pair, total, mate
            self.ss, self.rs = send_sem, recv_sem

        def at(self, slot):
            return self.buf.at[self.c, self.base + slot]

        def group(self, step):
            return self.buf.at[self.c, pl.ds(self.base + lax.rem(self.ring.place + step + 4, 4) * 2, 2)]

        def push(self, src, dst, kind, device):
            send(src, dst, self.ss.at[self.c, kind], self.rs.at[self.c, kind], device)

        def wait(self, dst, kind):
            await_recv(dst, self.ss.at[self.c, kind], self.rs.at[self.c, kind], self.ring.mate)

        def first(self):
            self.push(self.at(self.ring.slot(2, False)), self.near.at[self.c, 0], 0, self.ring.forward)
            self.push(self.at(self.ring.slot(2, True)), self.near.at[self.c, 1], 1, self.ring.backward)

        def second(self):
            for kind, step, other, device in ((0, 1, False, self.ring.forward), (1, -1, True, self.ring.backward)):
                self.wait(self.near.at[self.c, kind], kind)
                slot = self.base + self.ring.slot(step, other)
                self.buf[self.c, slot] = (
                    self.buf[self.c, slot].astype(jnp.float32) + self.near[self.c, kind].astype(jnp.float32)
                ).astype(jnp.bfloat16)
                self.push(self.group(step), self.pair.at[self.c, kind], 2 + kind, device)

        def three(self, bit):
            slot = self.base + self.ring.place * 2 + bit
            return (
                self.buf[self.c, slot].astype(jnp.float32)
                + self.pair[self.c, 0, bit].astype(jnp.float32)
                + self.pair[self.c, 1, bit].astype(jnp.float32)
            )

        def third(self):
            self.wait(self.pair.at[self.c, 0], 2)
            self.wait(self.pair.at[self.c, 1], 3)
            self.total[self.c] = self.three(1 - self.ring.bit).astype(jnp.bfloat16)
            self.push(self.total.at[self.c], self.mate.at[self.c], 4, self.ring.mate)

        def last(self):
            self.wait(self.mate.at[self.c], 4)
            return self.three(self.ring.bit) + self.mate[self.c].astype(jnp.float32)

    class Chunk:
        def __init__(self, c):
            self.c = c
            self.cols = slice(c * width, (c + 1) * width)
            self.mine = core * 8
            self.spread = Gather(c, col_ring, panel, self.mine, panel_send, panel_recv)
            self.back = Scatter(
                c, row_ring, back, 0, row_near, row_pair, row_sum, row_mate, row_send, row_recv
            )
            self.share = Gather(c, row_ring, hidden, 0, hidden_send, hidden_recv)
            self.ahead = Scatter(
                c, col_ring, ahead, self.mine, col_near, col_pair, col_sum, col_mate, col_send, col_recv
            )

        def to_partner(self, src, slot, kind):
            send(
                src, panel.at[self.c, self.mine + slot],
                core_send.at[self.c, kind], core_recv.at[self.c, kind], partner,
            )

        def pass_on(self, kinds):
            for kind in kinds:
                slot = self.spread.slots[kind]
                self.to_partner(self.spread.at(slot), slot, kind)

        def s0(self):
            own = features_ref.at[:, self.cols]
            self.spread.first(own)
            self.to_partner(own, col_ring.slot(0, False), 7)
            panel[self.c, self.mine + col_ring.slot(0, False)] = features_ref[:, self.cols]

        def s1(self):
            self.spread.second()
            self.pass_on([0])

        def s2(self):
            self.spread.third()
            self.pass_on([1, 2, 3, 4])

        def s3(self):
            self.spread.fourth()
            self.pass_on([5, 6])

        def s4(self):
            theirs = (1 - core) * 8
            slots = self.spread.slots + [col_ring.slot(0, False)]
            for kind in range(8):
                await_recv(
                    panel.at[self.c, theirs + slots[kind]],
                    core_send.at[self.c, kind], core_recv.at[self.c, kind], partner,
                )
            if self.c == 0:
                flipped_copy.wait()

            @pl.loop(0, 2)
            def _(i):
                lhs = flipped[pl.ds(pl.multiple_of(i * 512, 512), 512), :]
                part = jnp.dot(
                    lhs, panel[self.c].reshape(16 * PIECE, width), preferred_element_type=jnp.float32
                )
                back[self.c, pl.ds(i * 4, 4)] = part.astype(jnp.bfloat16).reshape(4, PIECE, width)

            self.back.first()

        def s5(self):
            self.back.second()

        def s6(self):
            self.back.third()

        def s7(self):
            sums = self.back.last()
            own = row_ring.slot(0, False)
            for k in range(width // CH):
                mixed = jnp.dot(
                    normalize(sums[:, k * CH : (k + 1) * CH]), mix_in_ref[...], preferred_element_type=jnp.float32
                )
                hidden[self.c, own, :, k * CH : (k + 1) * CH] = gelu(mixed).astype(jnp.bfloat16)
            self.share.first(self.share.at(own))

        def s8(self):
            self.share.second()

        def s9(self):
            self.share.third()

        def s10(self):
            self.share.fourth()
            if self.c == 0:
                block_copy.wait()

            @pl.loop(0, 4)
            def _(i):
                half = lax.rem(i // 2 + 1 - core + 2, 2)
                place = half * 2 + lax.rem(i, 2)
                lhs = block[pl.ds(pl.multiple_of(place * 512, 512), 512), :]
                part = jnp.dot(
                    lhs, hidden[self.c].reshape(8 * PIECE, width), preferred_element_type=jnp.float32
                )
                ahead[self.c, pl.ds(place * 4, 4)] = part.astype(jnp.bfloat16).reshape(4, PIECE, width)

            send(
                ahead.at[self.c, pl.ds((1 - core) * 8, 8)], across.at[self.c],
                swap_send.at[self.c], swap_recv.at[self.c], partner,
            )

        def s11(self):
            await_recv(across.at[self.c], swap_send.at[self.c], swap_recv.at[self.c], partner)

            @pl.loop(0, 8)
            def _(i):
                ahead[self.c, self.mine + i] = (
                    ahead[self.c, self.mine + i].astype(jnp.float32) + across[self.c, i].astype(jnp.float32)
                ).astype(jnp.bfloat16)

            self.ahead.first()

        def s12(self):
            self.ahead.second()

        def s13(self):
            self.ahead.third()

        def s14(self):
            sums = self.ahead.last()
            for k in range(width // CH):
                at = slice(self.c * width + k * CH, self.c * width + (k + 1) * CH)
                recon = jnp.dot(
                    normalize(sums[:, k * CH : (k + 1) * CH]), mix_out_ref[...], preferred_element_type=jnp.float32
                )
                out_ref[:, at] = features_ref[:, at].astype(jnp.float32) - recon

    chunks = [Chunk(c) for c in range(CHUNKS)]
    for tick in range(15 + LAG * (CHUNKS - 1)):
        for c in range(CHUNKS):
            stage = tick - LAG * c
            if 0 <= stage < 15:
                getattr(chunks[c], "s%d" % stage)()
    for copy in sent:
        copy.wait_send()


def two_hops(features, block, flipped, mix_in, mix_out):
    feat = features.shape[1]
    width = feat // CHUNKS
    dma = pltpu.SemaphoreType.DMA

    def buf(*shape):
        return pltpu.VMEM((CHUNKS,) + shape + (PIECE, width), jnp.bfloat16)

    vmem = pl.BlockSpec(memory_space=pltpu.VMEM)
    hbm = pl.BlockSpec(memory_space=pl.ANY)
    scatter = [buf(2), buf(2, 2), buf(), buf()]
    return pl.pallas_call(
        hops_kernel,
        out_shape=jax.ShapeDtypeStruct((PIECE, feat), jnp.float32),
        in_specs=[vmem, hbm, hbm, vmem, vmem],
        out_specs=vmem,
        scratch_shapes=[
            pltpu.VMEM(block.shape, jnp.bfloat16),
            pltpu.VMEM(flipped.shape, jnp.bfloat16),
            buf(16), buf(8), buf(8), buf(16), buf(8),
            *scatter, *scatter,
            dma((2,)),
            dma((CHUNKS, 7)), dma((CHUNKS, 7)),
            dma((CHUNKS, 8)), dma((CHUNKS, 8)),
            dma((CHUNKS, 7)), dma((CHUNKS, 7)),
            dma((CHUNKS, 5)), dma((CHUNKS, 5)),
            dma((CHUNKS, 5)), dma((CHUNKS, 5)),
            dma((CHUNKS,)), dma((CHUNKS,)),
        ],
        compiler_params=pltpu.CompilerParams(
            collective_id=0, has_side_effects=True, vmem_limit_bytes=60 << 20
        ),
        name="two_hops",
    )(features, block, flipped, mix_in, mix_out)


def local(ingest_features, node_map, unit_rows, tile_ids, tile_values, mix_in, mix_out):
    row_count = lax.axis_size("row")
    col_count = lax.axis_size("col")
    unit_count = row_count * col_count
    slots_held = node_map.shape[0]
    per_pair = slots_held // unit_count
    feature_width = ingest_features.shape[1]
    row_tiles = col_count * PIECE // TILE
    col_tiles = row_count * PIECE // TILE

    local_rows = tile_ids[:, 0] - lax.axis_index("row") * row_tiles
    local_cols = tile_ids[:, 1] - lax.axis_index("col") * col_tiles
    place = (lax.rem(local_rows, 2) * 4 + lax.rem(local_rows // 2, 4)) * 2 + local_rows // 8
    real = tile_ids[:, 0] < unit_count * PIECE // TILE
    spot = jnp.where(real, place * col_tiles + local_cols, -1)
    slot_ids = jnp.arange(tile_ids.shape[0], dtype=jnp.int32)
    slot_of = jnp.max(
        jnp.where(
            spot[None, :] == jnp.arange(row_tiles * col_tiles, dtype=jnp.int32)[:, None], slot_ids[None, :], -1
        ),
        axis=1,
    )
    block, flipped = build_block(slot_of, tile_values, row_tiles, col_tiles)

    owner = node_map // PIECE
    slot = jnp.arange(slots_held, dtype=jnp.int32)
    live = slot < unit_rows[0]
    same = (owner[:, None] == owner[None, :]) & live[None, :] & (slot[None, :] < slot[:, None])
    rank_within = jnp.sum(same.astype(jnp.int32), axis=1)
    target = jnp.where(live, owner * per_pair + rank_within, -1)
    pick = (target[None, :] == slot[:, None]).astype(jnp.bfloat16)
    marks = jnp.broadcast_to((node_map % PIECE + 1).astype(jnp.bfloat16)[:, None], (slots_held, CH))
    outgoing = jnp.dot(
        pick, jnp.concatenate([ingest_features, marks], axis=1), preferred_element_type=jnp.float32
    ).astype(jnp.bfloat16)
    arrived = lax.all_to_all(
        outgoing.reshape(unit_count, per_pair, feature_width + CH),
        ("row", "col"),
        split_axis=0,
        concat_axis=0,
        tiled=True,
    ).reshape(-1, feature_width + CH)
    arrived_at = arrived[:, feature_width].astype(jnp.int32) - 1
    put = (arrived_at[None, :] == jnp.arange(PIECE, dtype=jnp.int32)[:, None]).astype(jnp.bfloat16)
    features = jnp.dot(put, arrived[:, :feature_width], preferred_element_type=jnp.float32).astype(jnp.bfloat16)
    return two_hops(features, block, flipped, mix_in, mix_out)


def solution(mesh):
    return jax.shard_map(
        local,
        mesh=mesh,
        in_specs=(
            P(("row", "col"), None),
            P(("row", "col")),
            P(("row", "col")),
            P(("row", "col"), None),
            P(("row", "col"), None, None),
            P(),
            P(),
        ),
        out_specs=P(("row", "col"), None),
        check_vma=False,
    )
```

time: 345 us -> 160 us (0.46)
  waiting for transfers between devices: 244 us -> 6.2 us
  Pallas kernels: 0 us -> 133 us
  local copies, waits for them, and re-layouts: 40.2 us -> 3.77 us
  matrix products: 25.5 us -> 2.58 us
  between operations: 14 us -> 0.74 us
  starting transfers between devices: 16.4 us -> 11.1 us
    reduce_scatter x2 -> x0, waiting for transfers between devices: 149 us -> none  [the longest x1 80.5 us: local(): lax.psum_scatter(back_part.astype(jnp.bfloat16), 'row', scatter_dimension...]
    pallas_call x0 -> x2, Pallas kernels: none -> 133 us  [the longest x1 123 us: two_hops(): pl.pallas_call(hops_kernel, out_shape=jax.ShapeDtypeStruct((PIECE, feat),...]
    all_gather x2 -> x0, waiting for transfers between devices: 74.8 us -> none  [the longest x1 61.5 us: local(): hidden = lax.all_gather(encode(back_own, mix_in), 'row', axis=0, tiled=True)]
    dot_general x4 -> x2, matrix products: 25.5 us -> 2.58 us  [the longest x1 1.55 us: local(): jnp.dot(pick, jnp.concatenate([ingest_features, marks], axis=1), preferre...]
    scatter x4 -> x0, local copies, waits for them, and re-layouts: 21 us -> none  [the longest x1 13.7 us: dense_block(): tile_grid.at[local_rows, local_cols].set(tile_values, mode='drop')]
    all_to_all x2 -> x1, waiting for transfers between devices: 20.2 us -> 6.2 us  [local(): lax.all_to_all(outgoing.reshape(unit_count, per_pair, feature_width + CH)...]
    transpose x1 -> x0, local copies, waits for them, and re-layouts: 7.85 us -> none  [dense_block(): tile_grid.transpose(0, 2, 1, 3)]
    reshape x7 -> x2, local copies, waits for them, and re-layouts: 6.68 us -> 1.6 us  [the longest x1 1.28 us: local(): outgoing.reshape(unit_count, per_pair, feature_width + CH)]
  transfers between devices with their start and end apart: 6 -> 1, of which waited for: 6 -> 1; matrix products, arithmetic and copies ran while one was open for 9% -> 0% of each run, Pallas kernels for 0% -> 6%
where the time goes in v1:
time: 160 us; the launch traced here: 159 us
  Pallas kernels  133 us (83%)
  starting transfers between devices  11.1 us (7%)
  waiting for transfers between devices  6.2 us (4%)
  local copies, waits for them, and re-layouts  3.77 us (2%)
  matrix products  2.58 us (2%)
  other arithmetic  1.63 us (1%)
    pallas_call x1, Pallas kernels, two_hops(): pl.pallas_call(hops_kernel, out_shape=jax.ShapeDtypeStruct((PIECE, feat),...  123 us
    all_to_all x1, starting transfers between devices, local(): lax.all_to_all(outgoing.reshape(unit_count, per_pair, feature_width + CH)...  11.1 us
    pallas_call x1, Pallas kernels, build_block(): pl.pallas_call(block_kernel, grid_spec=pltpu.PrefetchScalarGridSpec(num_s...  10.1 us
    all_to_all x1, waiting for transfers between devices, local(): lax.all_to_all(outgoing.reshape(unit_count, per_pair, feature_width + CH)...  6.2 us
  transfers between devices with their start and end apart: 1, of which 1 were waited for; matrix products, arithmetic and copies ran while one was open for 0% of the time, Pallas kernels for 6%

profile of v1, /device:TPU:0, one launch (start us, length us, event | category | flops | bytes accessed | tf_op | source)
XLA Modules:
  0.0 159.2 jit_solution(6077023033279372040)
XLA Ops:
  0.7 0.7 and_select_fusion.3
  1.4 0.2 convert_reduce_fusion
  1.6 0.1 broadcast_in_dim.17
  1.7 1.5 convolution_convert_fusion
  3.2 0.0 copy-start
  3.2 1.3 reshape.81
  4.5 11.1 %all-to-all-start = ((bf16[128,2,1664]{2,1,0:T(2,128)(2,1)}), bf16[128,2,1664]{2,1,0:T(2,128)(2,1)S(1)}, u32[]{:S(2)}, u32[]{:S(2)}) async-start(bf16[128,2,1664]{2,1,0:T(2,128)(2,1)} %reshape.81), calls=%async_computation | async-start | bytes 1703936 | tf_op jit(solution)/shard_map/all_to_all | solution.py:426
  15.7 0.0 copy-done
  15.7 0.6 select_reduce_fusion.slot_ref
  16.3 10.1 %build_block.1 = (bf16[2048,1024]{1,0:T(8,128)(2,1)}, bf16[1024,2048]{1,0:T(8,128)(2,1)}) custom-call(s32[128]{0:T(128)} %select_reduce_fusion.slot_ref, bf16[96,128,128]{2,1,0:T(8,128)(2,1)} %tiles_ref.1), custom_call_target="tpu_custom_call" | custom-call | bytes 25165824 | tf_op jit(solution)/shard_map/build_block/pallas_call | solution.py:51
  26.5 6.2 %all-to-all-done = bf16[128,2,1664]{2,1,0:T(2,128)(2,1)S(1)} async-done(((bf16[128,2,1664]{2,1,0:T(2,128)(2,1)}), bf16[128,2,1664]{2,1,0:T(2,128)(2,1)S(1)}, u32[]{:S(2)}, u32[]{:S(2)}) %all-to-all-start) | async-done | bytes 852000 | tf_op jit(solution)/shard_map/all_to_all | solution.py:426
  32.7 0.3 reshape.82
  33.0 0.1 add_reduce_fusion
  33.1 1.0 convolution_convert_fusion.1.features_ref
  34.1 123.0 %two_hops.1 = f32[128,1536]{1,0:T(8,128)} custom-call(bf16[128,1536]{1,0:T(8,128)(2,1)} %convolution_convert_fusion.1.features_ref, bf16[2048,1024]{1,0:T(8,128)(2,1)} %get-tuple-element.7.block_hbm, bf16[1024,2048]{1,0:T(8,128)(2,1)} %get-tuple-element.8.flipped_hbm, bf16[128,128]{1,0:T(8,128)(2,1)} %mix_in_ref.1, bf16[128,128]{1,0:T(8,128)(2,1)} %mix_out_ref.1), custom_call_target="tpu_custom_call" | custom-call | tf_op jit(solution)/shard_map/two_hops/pallas_call | solution.py:366
  157.1 2.1 %copy.11 = f32[128,1536]{1,0:T(8,128)} copy(f32[128,1536]{1,0:T(8,128)} %two_hops.1) | data formatting | bytes 1572864
  (3 shorter events, 0.0 us)
Async XLA Ops:
  3.2 12.4 %copy-start = (s32[96,2]{0,1:T(2,128)S(1)}, s32[96,2]{0,1:T(2,128)}, u32[]{:S(2)}) copy-start(s32[96,2]{0,1:T(2,128)} %param.10) | copy-start | bytes 2308
  4.5 28.1 %all-to-all-start = ((bf16[128,2,1664]{2,1,0:T(2,128)(2,1)}), bf16[128,2,1664]{2,1,0:T(2,128)(2,1)S(1)}, u32[]{:S(2)}, u32[]{:S(2)}) async-start(bf16[128,2,1664]{2,1,0:T(2,128)(2,1)} %reshape.81), calls=%async_computation | async-start | bytes 1703936 | tf_op jit(solution)/shard_map/all_to_all | solution.py:426

commit v2 on v1

--- a/solution.py
+++ b/solution.py
@@ -10,8 +10,22 @@
 CH = 128
 TILE = 128
 PIECE = 128
-CHUNKS = 3
-LAG = 3
+CHUNKS = 6
+ORDER = (
+    (0, 0), (1, 0), (2, 0), (0, 3), (0, 2), (0, 1), (1, 3), (1, 2), (1, 1), (2, 3), (2, 2), (2, 1), (0, 6), (0, 5),
+    (0, 4), (1, 5), (1, 6), (2, 5), (0, 7), (1, 4), (3, 0), (0, 8), (1, 7), (2, 7), (2, 6), (2, 4), (4, 0), (1, 8),
+    (3, 3), (3, 2), (3, 1), (0, 10), (0, 9), (4, 3), (4, 2), (4, 1), (2, 8), (5, 0), (1, 10), (1, 9), (3, 6),
+    (3, 5), (3, 4), (4, 5), (0, 11), (4, 6), (5, 3), (5, 1), (2, 10), (2, 9), (3, 7), (4, 4), (5, 2), (3, 8),
+    (1, 11), (4, 7), (5, 5), (5, 4), (0, 12), (5, 6), (4, 8), (2, 11), (5, 7), (3, 10), (3, 9), (5, 8), (0, 15),
+    (0, 14), (1, 12), (4, 10), (4, 9), (0, 13), (3, 11), (5, 10), (5, 9), (2, 12), (0, 18), (1, 15), (1, 14),
+    (1, 13), (0, 17), (4, 11), (3, 12), (0, 16), (2, 13), (2, 15), (5, 11), (1, 17), (2, 14), (4, 12), (0, 19),
+    (1, 18), (0, 20), (1, 16), (3, 15), (3, 13), (2, 17), (3, 14), (1, 19), (2, 16), (1, 20), (0, 21), (2, 18),
+    (4, 15), (5, 12), (3, 17), (4, 14), (4, 13), (2, 19), (3, 16), (2, 20), (0, 23), (0, 22), (1, 21), (3, 18),
+    (5, 15), (5, 14), (3, 19), (3, 20), (2, 21), (4, 18), (4, 17), (4, 16), (5, 13), (0, 24), (5, 18), (1, 23),
+    (1, 22), (3, 21), (2, 23), (2, 22), (4, 19), (5, 16), (4, 20), (0, 25), (5, 17), (1, 24), (3, 23), (3, 22),
+    (4, 21), (5, 19), (5, 20), (1, 25), (2, 24), (3, 24), (5, 21), (4, 23), (2, 25), (4, 22), (3, 25), (5, 23),
+    (5, 22), (4, 24), (5, 24), (4, 25), (5, 25),
+)
 MESH = pl.DeviceIdType.MESH
 
 epsilon = 1e-05
@@ -149,17 +163,13 @@
             self.push(self.at(slot), slot, 3, self.ring.forward)
             self.push(self.at(slot), slot, 4, self.ring.backward)
 
-        def third(self, also=None):
-            self.wait(1)
-            self.push(self.at(self.slots[1]), self.slots[1], 5, self.ring.forward)
-            self.wait(2)
-            self.wait(4)
-            self.push(self.at(self.slots[4]), self.slots[4], 6, self.ring.backward)
-            self.wait(3)
-
-        def fourth(self):
-            self.wait(5)
-            self.wait(6)
+        def relay(self, kind):
+            self.wait(kind)
+            slot = self.slots[kind]
+            if kind == 1:
+                self.push(self.at(slot), slot, 5, self.ring.forward)
+            if kind == 4:
+                self.push(self.at(slot), slot, 6, self.ring.backward)
 
     class Scatter:
         def __init__(self, c, ring, buf, base, near, pair, total, mate, send_sem, recv_sem):
@@ -183,14 +193,14 @@
             self.push(self.at(self.ring.slot(2, False)), self.near.at[self.c, 0], 0, self.ring.forward)
             self.push(self.at(self.ring.slot(2, True)), self.near.at[self.c, 1], 1, self.ring.backward)
 
-        def second(self):
-            for kind, step, other, device in ((0, 1, False, self.ring.forward), (1, -1, True, self.ring.backward)):
-                self.wait(self.near.at[self.c, kind], kind)
-                slot = self.base + self.ring.slot(step, other)
-                self.buf[self.c, slot] = (
-                    self.buf[self.c, slot].astype(jnp.float32) + self.near[self.c, kind].astype(jnp.float32)
-                ).astype(jnp.bfloat16)
-                self.push(self.group(step), self.pair.at[self.c, kind], 2 + kind, device)
+        def second(self, kind):
+            step, other, device = ((1, False, self.ring.forward), (-1, True, self.ring.backward))[kind]
+            self.wait(self.near.at[self.c, kind], kind)
+            slot = self.base + self.ring.slot(step, other)
+            self.buf[self.c, slot] = (
+                self.buf[self.c, slot].astype(jnp.float32) + self.near[self.c, kind].astype(jnp.float32)
+            ).astype(jnp.bfloat16)
+            self.push(self.group(step), self.pair.at[self.c, kind], 2 + kind, device)
 
         def three(self, bit):
             slot = self.base + self.ring.place * 2 + bit
@@ -230,30 +240,25 @@
                 core_send.at[self.c, kind], core_recv.at[self.c, kind], partner,
             )
 
-        def pass_on(self, kinds):
-            for kind in kinds:
-                slot = self.spread.slots[kind]
-                self.to_partner(self.spread.at(slot), slot, kind)
-
-        def s0(self):
+        def pass_on(self, kind):
+            slot = self.spread.slots[kind]
+            self.to_partner(self.spread.at(slot), slot, kind)
+
+        def begin(self):
             own = features_ref.at[:, self.cols]
             self.spread.first(own)
             self.to_partner(own, col_ring.slot(0, False), 7)
             panel[self.c, self.mine + col_ring.slot(0, False)] = features_ref[:, self.cols]
 
-        def s1(self):
+        def spread_mate(self):
             self.spread.second()
-            self.pass_on([0])
-
-        def s2(self):
-            self.spread.third()
-            self.pass_on([1, 2, 3, 4])
-
-        def s3(self):
-            self.spread.fourth()
-            self.pass_on([5, 6])
-
-        def s4(self):
+            self.pass_on(0)
+
+        def spread_relay(self, kind):
+            self.spread.relay(kind)
+            self.pass_on(kind)
+
+        def back_product(self):
             theirs = (1 - core) * 8
             slots = self.spread.slots + [col_ring.slot(0, False)]
             for kind in range(8):
@@ -274,13 +279,7 @@
 
             self.back.first()
 
-        def s5(self):
-            self.back.second()
-
-        def s6(self):
-            self.back.third()
-
-        def s7(self):
+        def encode(self):
             sums = self.back.last()
             own = row_ring.slot(0, False)
             for k in range(width // CH):
@@ -290,14 +289,7 @@
                 hidden[self.c, own, :, k * CH : (k + 1) * CH] = gelu(mixed).astype(jnp.bfloat16)
             self.share.first(self.share.at(own))
 
-        def s8(self):
-            self.share.second()
-
-        def s9(self):
-            self.share.third()
-
-        def s10(self):
-            self.share.fourth()
+        def ahead_product(self):
             if self.c == 0:
                 block_copy.wait()
 
@@ -316,7 +308,7 @@
                 swap_send.at[self.c], swap_recv.at[self.c], partner,
             )
 
-        def s11(self):
+        def join_cores(self):
             await_recv(across.at[self.c], swap_send.at[self.c], swap_recv.at[self.c], partner)
 
             @pl.loop(0, 8)
@@ -327,13 +319,7 @@
 
             self.ahead.first()
 
-        def s12(self):
-            self.ahead.second()
-
-        def s13(self):
-            self.ahead.third()
-
-        def s14(self):
+        def decode(self):
             sums = self.ahead.last()
             for k in range(width // CH):
                 at = slice(self.c * width + k * CH, self.c * width + (k + 1) * CH)
@@ -342,12 +328,30 @@
                 )
                 out_ref[:, at] = features_ref[:, at].astype(jnp.float32) - recon
 
-    chunks = [Chunk(c) for c in range(CHUNKS)]
-    for tick in range(15 + LAG * (CHUNKS - 1)):
-        for c in range(CHUNKS):
-            stage = tick - LAG * c
-            if 0 <= stage < 15:
-                getattr(chunks[c], "s%d" % stage)()
+        def steps(self):
+            part = functools.partial
+            return [
+                self.begin,
+                self.spread_mate,
+                *[part(self.spread_relay, kind) for kind in range(1, 7)],
+                self.back_product,
+                part(self.back.second, 0),
+                part(self.back.second, 1),
+                self.back.third,
+                self.encode,
+                self.share.second,
+                *[part(self.share.relay, kind) for kind in range(1, 7)],
+                self.ahead_product,
+                self.join_cores,
+                part(self.ahead.second, 0),
+                part(self.ahead.second, 1),
+                self.ahead.third,
+                self.decode,
+            ]
+
+    steps = [Chunk(c).steps() for c in range(CHUNKS)]
+    for c, step in ORDER:
+        steps[c][step]()
     for copy in sent:
         copy.wait_send()
 

time: 160 us -> 138 us (0.86)
  Pallas kernels: 133 us -> 112 us
    pallas_call x1, Pallas kernels: 123 us -> 102 us  [two_hops(): pl.pallas_call(hops_kernel, out_shape=jax.ShapeDtypeStruct((PIECE, feat),...]
  transfers between devices with their start and end apart: 1 -> 1, of which waited for: 1 -> 1; matrix products, arithmetic and copies ran while one was open for 0% -> 0% of each run, Pallas kernels for 6% -> 7%
where the time goes in v2:
time: 138 us
  Pallas kernels  112 us (81%)
  starting transfers between devices  11.1 us (8%)
  waiting for transfers between devices  6.2 us (4%)
  local copies, waits for them, and re-layouts  3.77 us (3%)
  matrix products  2.58 us (2%)
  other arithmetic  1.63 us (1%)
    pallas_call x1, Pallas kernels, two_hops(): pl.pallas_call(hops_kernel, out_shape=jax.ShapeDtypeStruct((PIECE, feat),...  102 us
    all_to_all x1, starting transfers between devices, local(): lax.all_to_all(outgoing.reshape(unit_count, per_pair, feature_width + CH)...  11.1 us
    pallas_call x1, Pallas kernels, build_block(): pl.pallas_call(block_kernel, grid_spec=pltpu.PrefetchScalarGridSpec(num_s...  10.1 us
    all_to_all x1, waiting for transfers between devices, local(): lax.all_to_all(outgoing.reshape(unit_count, per_pair, feature_width + CH)...  6.2 us
  transfers between devices with their start and end apart: 1, of which 1 were waited for; matrix products, arithmetic and copies ran while one was open for 0% of the time, Pallas kernels for 7%

profile of v2, /device:TPU:0, one launch (start us, length us, event | category | flops | bytes accessed | tf_op | source)
XLA Modules:
  0.0 137.9 jit_solution(15028301608837175109)
XLA Ops:
  0.7 0.7 and_select_fusion.3
  1.4 0.2 convert_reduce_fusion
  1.6 0.1 broadcast_in_dim.17
  1.7 1.5 %convolution_convert_fusion = bf16[256,1664]{1,0:T(8,128)(2,1)S(1)} fusion(bf16[256,128]{1,0:T(8,128)(2,1)S(1)} %broadcast_in_dim.17, bf16[256,1536]{1,0:T(8,128)(2,1)} %param.7, s32[256]{0:T(256)S(1)} %add_select_fusion), kind=kOutput, calls=%fused_computation | convolution fusion | flops 220299264 | bytes 1704960 | tf_op jit(solution)/shard_map/dot_general | solution.py:427
  3.2 0.0 copy-start
  3.2 1.3 reshape.81
  4.5 11.1 %all-to-all-start = ((bf16[128,2,1664]{2,1,0:T(2,128)(2,1)}), bf16[128,2,1664]{2,1,0:T(2,128)(2,1)S(1)}, u32[]{:S(2)}, u32[]{:S(2)}) async-start(bf16[128,2,1664]{2,1,0:T(2,128)(2,1)} %reshape.81), calls=%async_computation | async-start | bytes 1703936 | tf_op jit(solution)/shard_map/all_to_all | solution.py:430
  15.7 0.0 copy-done
  15.7 0.6 select_reduce_fusion.slot_ref
  16.3 10.1 %build_block.1 = (bf16[2048,1024]{1,0:T(8,128)(2,1)}, bf16[1024,2048]{1,0:T(8,128)(2,1)}) custom-call(s32[128]{0:T(128)} %select_reduce_fusion.slot_ref, bf16[96,128,128]{2,1,0:T(8,128)(2,1)} %tiles_ref.1), custom_call_target="tpu_custom_call" | custom-call | bytes 25165824 | tf_op jit(solution)/shard_map/build_block/pallas_call | solution.py:65
  26.5 6.2 %all-to-all-done = bf16[128,2,1664]{2,1,0:T(2,128)(2,1)S(1)} async-done(((bf16[128,2,1664]{2,1,0:T(2,128)(2,1)}), bf16[128,2,1664]{2,1,0:T(2,128)(2,1)S(1)}, u32[]{:S(2)}, u32[]{:S(2)}) %all-to-all-start) | async-done | bytes 852000 | tf_op jit(solution)/shard_map/all_to_all | solution.py:430
  32.7 0.3 reshape.82
  33.0 0.1 add_reduce_fusion
  33.1 1.0 convolution_convert_fusion.1.features_ref
  34.1 101.7 %two_hops.1 = f32[128,1536]{1,0:T(8,128)} custom-call(bf16[128,1536]{1,0:T(8,128)(2,1)} %convolution_convert_fusion.1.features_ref, bf16[2048,1024]{1,0:T(8,128)(2,1)} %get-tuple-element.7.block_hbm, bf16[1024,2048]{1,0:T(8,128)(2,1)} %get-tuple-element.8.flipped_hbm, bf16[128,128]{1,0:T(8,128)(2,1)} %mix_in_ref.1, bf16[128,128]{1,0:T(8,128)(2,1)} %mix_out_ref.1), custom_call_target="tpu_custom_call" | custom-call | tf_op jit(solution)/shard_map/two_hops/pallas_call | solution.py:370
  135.8 2.1 %copy.11 = f32[128,1536]{1,0:T(8,128)} copy(f32[128,1536]{1,0:T(8,128)} %two_hops.1) | data formatting | bytes 1572864
  (3 shorter events, 0.0 us)
Async XLA Ops:
  3.2 12.4 %copy-start = (s32[96,2]{0,1:T(2,128)S(1)}, s32[96,2]{0,1:T(2,128)}, u32[]{:S(2)}) copy-start(s32[96,2]{0,1:T(2,128)} %param.10) | copy-start | bytes 2308
  4.5 28.1 %all-to-all-start = ((bf16[128,2,1664]{2,1,0:T(2,128)(2,1)}), bf16[128,2,1664]{2,1,0:T(2,128)(2,1)S(1)}, u32[]{:S(2)}, u32[]{:S(2)}) async-start(bf16[128,2,1664]{2,1,0:T(2,128)(2,1)} %reshape.81), calls=%async_computation | async-start | bytes 1703936 | tf_op jit(solution)/shard_map/all_to_all | solution.py:430

commit v3 on v2

--- a/solution.py
+++ b/solution.py
@@ -12,19 +12,19 @@
 PIECE = 128
 CHUNKS = 6
 ORDER = (
-    (0, 0), (1, 0), (2, 0), (0, 3), (0, 2), (0, 1), (1, 3), (1, 2), (1, 1), (2, 3), (2, 2), (2, 1), (0, 6), (0, 5),
-    (0, 4), (1, 5), (1, 6), (2, 5), (0, 7), (1, 4), (3, 0), (0, 8), (1, 7), (2, 7), (2, 6), (2, 4), (4, 0), (1, 8),
-    (3, 3), (3, 2), (3, 1), (0, 10), (0, 9), (4, 3), (4, 2), (4, 1), (2, 8), (5, 0), (1, 10), (1, 9), (3, 6),
-    (3, 5), (3, 4), (4, 5), (0, 11), (4, 6), (5, 3), (5, 1), (2, 10), (2, 9), (3, 7), (4, 4), (5, 2), (3, 8),
-    (1, 11), (4, 7), (5, 5), (5, 4), (0, 12), (5, 6), (4, 8), (2, 11), (5, 7), (3, 10), (3, 9), (5, 8), (0, 15),
-    (0, 14), (1, 12), (4, 10), (4, 9), (0, 13), (3, 11), (5, 10), (5, 9), (2, 12), (0, 18), (1, 15), (1, 14),
-    (1, 13), (0, 17), (4, 11), (3, 12), (0, 16), (2, 13), (2, 15), (5, 11), (1, 17), (2, 14), (4, 12), (0, 19),
-    (1, 18), (0, 20), (1, 16), (3, 15), (3, 13), (2, 17), (3, 14), (1, 19), (2, 16), (1, 20), (0, 21), (2, 18),
-    (4, 15), (5, 12), (3, 17), (4, 14), (4, 13), (2, 19), (3, 16), (2, 20), (0, 23), (0, 22), (1, 21), (3, 18),
-    (5, 15), (5, 14), (3, 19), (3, 20), (2, 21), (4, 18), (4, 17), (4, 16), (5, 13), (0, 24), (5, 18), (1, 23),
-    (1, 22), (3, 21), (2, 23), (2, 22), (4, 19), (5, 16), (4, 20), (0, 25), (5, 17), (1, 24), (3, 23), (3, 22),
-    (4, 21), (5, 19), (5, 20), (1, 25), (2, 24), (3, 24), (5, 21), (4, 23), (2, 25), (4, 22), (3, 25), (5, 23),
-    (5, 22), (4, 24), (5, 24), (4, 25), (5, 25),
+    (0, 0), (1, 0), (0, 1), (0, 2), (0, 3), (1, 1), (1, 2), (1, 3), (2, 0), (0, 5), (0, 4), (0, 6), (1, 5), (2, 1),
+    (3, 0), (1, 4), (2, 3), (1, 6), (0, 7), (3, 1), (1, 7), (2, 2), (0, 8), (2, 5), (2, 4), (1, 8), (3, 2), (3, 3),
+    (3, 5), (3, 4), (0, 10), (0, 9), (2, 6), (2, 7), (4, 0), (5, 0), (1, 10), (3, 6), (1, 9), (3, 7), (2, 8),
+    (4, 1), (3, 8), (5, 1), (0, 11), (4, 2), (5, 2), (4, 3), (5, 3), (4, 5), (4, 4), (1, 11), (2, 10), (2, 9),
+    (5, 5), (5, 4), (3, 10), (3, 9), (4, 6), (4, 7), (0, 12), (5, 6), (4, 8), (5, 7), (1, 12), (2, 11), (5, 8),
+    (0, 13), (3, 11), (0, 14), (0, 15), (4, 10), (4, 9), (1, 13), (1, 14), (1, 15), (5, 10), (5, 9), (2, 12),
+    (0, 17), (0, 16), (0, 18), (3, 12), (1, 17), (4, 11), (2, 13), (1, 16), (1, 18), (3, 13), (2, 15), (5, 11),
+    (0, 19), (0, 20), (4, 12), (2, 14), (3, 14), (1, 19), (1, 20), (0, 21), (2, 17), (5, 12), (3, 17), (2, 16),
+    (3, 16), (3, 15), (1, 21), (0, 23), (2, 18), (0, 22), (4, 13), (4, 14), (2, 19), (2, 20), (3, 18), (1, 23),
+    (1, 22), (5, 13), (5, 14), (3, 19), (3, 20), (4, 17), (2, 21), (4, 18), (4, 16), (5, 17), (4, 15), (5, 15),
+    (0, 24), (5, 16), (3, 21), (5, 18), (2, 23), (2, 22), (4, 19), (4, 20), (3, 23), (3, 22), (5, 19), (5, 20),
+    (4, 21), (1, 24), (2, 24), (5, 21), (4, 23), (4, 22), (5, 23), (5, 22), (3, 24), (4, 24), (5, 24), (0, 25),
+    (1, 25), (2, 25), (3, 25), (4, 25), (5, 25),
 )
 MESH = pl.DeviceIdType.MESH
 
@@ -326,7 +326,7 @@
                 recon = jnp.dot(
                     normalize(sums[:, k * CH : (k + 1) * CH]), mix_out_ref[...], preferred_element_type=jnp.float32
                 )
-                out_ref[:, at] = features_ref[:, at].astype(jnp.float32) - recon
+                out_ref[:, at] = recon
 
         def steps(self):
             part = functools.partial
@@ -437,7 +437,7 @@
     arrived_at = arrived[:, feature_width].astype(jnp.int32) - 1
     put = (arrived_at[None, :] == jnp.arange(PIECE, dtype=jnp.int32)[:, None]).astype(jnp.bfloat16)
     features = jnp.dot(put, arrived[:, :feature_width], preferred_element_type=jnp.float32).astype(jnp.bfloat16)
-    return two_hops(features, block, flipped, mix_in, mix_out)
+    return features.astype(jnp.float32) - two_hops(features, block, flipped, mix_in, mix_out)
 
 
 def solution(mesh):

time: 138 us -> 134 us (0.971)
  Pallas kernels: 112 us -> 107 us
  other arithmetic: 1.63 us -> 3.72 us
  local copies, waits for them, and re-layouts: 3.77 us -> 1.71 us
    pallas_call x1, Pallas kernels: 102 us -> 97.2 us  [two_hops(): pl.pallas_call(hops_kernel, out_shape=jax.ShapeDtypeStruct((PIECE, feat),...]
    sub x0 -> x1, other arithmetic: none -> 2.09 us  [local(): features.astype(jnp.float32)]
    unnamed x3 -> x4, local copies, waits for them, and re-layouts: 2.08 us -> 0.01 us
  transfers between devices with their start and end apart: 1 -> 1, of which waited for: 1 -> 1; matrix products, arithmetic and copies ran while one was open for 0% -> 0% of each run, Pallas kernels for 7% -> 8%
where the time goes in v3:
time: 134 us; the launch traced here: 133 us
  Pallas kernels  107 us (80%)
  starting transfers between devices  11.1 us (8%)
  waiting for transfers between devices  6.2 us (5%)
  other arithmetic  3.72 us (3%)
  matrix products  2.58 us (2%)
  local copies, waits for them, and re-layouts  1.71 us (1%)
    pallas_call x1, Pallas kernels, two_hops(): pl.pallas_call(hops_kernel, out_shape=jax.ShapeDtypeStruct((PIECE, feat),...  97.2 us
    all_to_all x1, starting transfers between devices, local(): lax.all_to_all(outgoing.reshape(unit_count, per_pair, feature_width + CH)...  11.1 us
    pallas_call x1, Pallas kernels, build_block(): pl.pallas_call(block_kernel, grid_spec=pltpu.PrefetchScalarGridSpec(num_s...  10.1 us
    all_to_all x1, waiting for transfers between devices, local(): lax.all_to_all(outgoing.reshape(unit_count, per_pair, feature_width + CH)...  6.2 us
  transfers between devices with their start and end apart: 1, of which 1 were waited for; matrix products, arithmetic and copies ran while one was open for 0% of the time, Pallas kernels for 8%

profile of v3, /device:TPU:0, one launch (start us, length us, event | category | flops | bytes accessed | tf_op | source)
XLA Modules:
  0.0 133.4 jit_solution(7177456710944758034)
XLA Ops:
  0.7 0.7 and_select_fusion.3
  1.4 0.2 convert_reduce_fusion
  1.6 0.1 broadcast_in_dim.17
  1.7 1.5 %convolution_convert_fusion = bf16[256,1664]{1,0:T(8,128)(2,1)S(1)} fusion(bf16[256,128]{1,0:T(8,128)(2,1)S(1)} %broadcast_in_dim.17, bf16[256,1536]{1,0:T(8,128)(2,1)} %param.7, s32[256]{0:T(256)S(1)} %add_select_fusion), kind=kOutput, calls=%fused_computation | convolution fusion | flops 220299264 | bytes 1704960 | tf_op jit(solution)/shard_map/dot_general | solution.py:427
  3.2 0.0 copy-start.1
  3.2 1.3 reshape.81
  4.5 11.1 %all-to-all-start = ((bf16[128,2,1664]{2,1,0:T(2,128)(2,1)}), bf16[128,2,1664]{2,1,0:T(2,128)(2,1)S(1)}, u32[]{:S(2)}, u32[]{:S(2)}) async-start(bf16[128,2,1664]{2,1,0:T(2,128)(2,1)} %reshape.81), calls=%async_computation | async-start | bytes 1703936 | tf_op jit(solution)/shard_map/all_to_all | solution.py:430
  15.7 0.0 copy-done.1
  15.7 0.6 select_reduce_fusion.slot_ref
  16.3 10.1 %build_block.1 = (bf16[2048,1024]{1,0:T(8,128)(2,1)}, bf16[1024,2048]{1,0:T(8,128)(2,1)}) custom-call(s32[128]{0:T(128)} %select_reduce_fusion.slot_ref, bf16[96,128,128]{2,1,0:T(8,128)(2,1)} %tiles_ref.1), custom_call_target="tpu_custom_call" | custom-call | bytes 25165824 | tf_op jit(solution)/shard_map/build_block/pallas_call | solution.py:65
  26.5 6.2 %all-to-all-done = bf16[128,2,1664]{2,1,0:T(2,128)(2,1)S(1)} async-done(((bf16[128,2,1664]{2,1,0:T(2,128)(2,1)}), bf16[128,2,1664]{2,1,0:T(2,128)(2,1)S(1)}, u32[]{:S(2)}, u32[]{:S(2)}) %all-to-all-start) | async-done | bytes 852000 | tf_op jit(solution)/shard_map/all_to_all | solution.py:430
  32.7 0.3 reshape.82
  33.0 0.1 add_reduce_fusion
  33.1 1.0 convolution_convert_fusion.1.features_ref
  34.1 0.0 copy-start
  34.1 97.2 %two_hops.1 = f32[128,1536]{1,0:T(8,128)} custom-call(bf16[128,1536]{1,0:T(8,128)(2,1)} %convolution_convert_fusion.1.features_ref, bf16[2048,1024]{1,0:T(8,128)(2,1)} %get-tuple-element.7.block_hbm, bf16[1024,2048]{1,0:T(8,128)(2,1)} %get-tuple-element.8.flipped_hbm, bf16[128,128]{1,0:T(8,128)(2,1)} %mix_in_ref.1, bf16[128,128]{1,0:T(8,128)(2,1)} %mix_out_ref.1), custom_call_target="tpu_custom_call" | custom-call | tf_op jit(solution)/shard_map/two_hops/pallas_call | solution.py:370
  131.3 0.0 copy-done
  131.4 2.1 %convert_subtract_fusion = f32[128,1536]{1,0:T(8,128)} fusion(f32[128,1536]{1,0:T(8,128)} %two_hops.1, bf16[128,1536]{1,0:T(8,128)(2,1)S(1)} %copy-done), kind=kLoop, calls=%fused_computation.6 | loop fusion | flops 393216 | bytes 1966080 | tf_op jit(solution)/shard_map/sub | solution.py:440
  (3 shorter events, 0.0 us)
Async XLA Ops:
  3.2 12.4 %copy-start.1 = (s32[96,2]{0,1:T(2,128)S(1)}, s32[96,2]{0,1:T(2,128)}, u32[]{:S(2)}) copy-start(s32[96,2]{0,1:T(2,128)} %param.10) | copy-start | bytes 2308
  4.5 28.1 %all-to-all-start = ((bf16[128,2,1664]{2,1,0:T(2,128)(2,1)}), bf16[128,2,1664]{2,1,0:T(2,128)(2,1)S(1)}, u32[]{:S(2)}, u32[]{:S(2)}) async-start(bf16[128,2,1664]{2,1,0:T(2,128)(2,1)} %reshape.81), calls=%async_computation | async-start | bytes 1703936 | tf_op jit(solution)/shard_map/all_to_all | solution.py:430
  34.1 97.2 %copy-start = (bf16[128,1536]{1,0:T(8,128)(2,1)S(1)}, bf16[128,1536]{1,0:T(8,128)(2,1)}, u32[]{:S(2)}) copy-start(bf16[128,1536]{1,0:T(8,128)(2,1)} %convolution_convert_fusion.1.features_ref) | copy-start | bytes 1179652

commit v4 on v3

--- a/solution.py
+++ b/solution.py
@@ -12,18 +12,18 @@
 PIECE = 128
 CHUNKS = 6
 ORDER = (
-    (0, 0), (1, 0), (0, 1), (0, 2), (0, 3), (1, 1), (1, 2), (1, 3), (2, 0), (0, 5), (0, 4), (0, 6), (1, 5), (2, 1),
-    (3, 0), (1, 4), (2, 3), (1, 6), (0, 7), (3, 1), (1, 7), (2, 2), (0, 8), (2, 5), (2, 4), (1, 8), (3, 2), (3, 3),
-    (3, 5), (3, 4), (0, 10), (0, 9), (2, 6), (2, 7), (4, 0), (5, 0), (1, 10), (3, 6), (1, 9), (3, 7), (2, 8),
-    (4, 1), (3, 8), (5, 1), (0, 11), (4, 2), (5, 2), (4, 3), (5, 3), (4, 5), (4, 4), (1, 11), (2, 10), (2, 9),
-    (5, 5), (5, 4), (3, 10), (3, 9), (4, 6), (4, 7), (0, 12), (5, 6), (4, 8), (5, 7), (1, 12), (2, 11), (5, 8),
-    (0, 13), (3, 11), (0, 14), (0, 15), (4, 10), (4, 9), (1, 13), (1, 14), (1, 15), (5, 10), (5, 9), (2, 12),
-    (0, 17), (0, 16), (0, 18), (3, 12), (1, 17), (4, 11), (2, 13), (1, 16), (1, 18), (3, 13), (2, 15), (5, 11),
-    (0, 19), (0, 20), (4, 12), (2, 14), (3, 14), (1, 19), (1, 20), (0, 21), (2, 17), (5, 12), (3, 17), (2, 16),
-    (3, 16), (3, 15), (1, 21), (0, 23), (2, 18), (0, 22), (4, 13), (4, 14), (2, 19), (2, 20), (3, 18), (1, 23),
-    (1, 22), (5, 13), (5, 14), (3, 19), (3, 20), (4, 17), (2, 21), (4, 18), (4, 16), (5, 17), (4, 15), (5, 15),
-    (0, 24), (5, 16), (3, 21), (5, 18), (2, 23), (2, 22), (4, 19), (4, 20), (3, 23), (3, 22), (5, 19), (5, 20),
-    (4, 21), (1, 24), (2, 24), (5, 21), (4, 23), (4, 22), (5, 23), (5, 22), (3, 24), (4, 24), (5, 24), (0, 25),
+    (0, 0), (1, 0), (2, 0), (0, 1), (0, 3), (0, 2), (1, 1), (1, 3), (1, 2), (2, 1), (2, 3), (2, 2), (0, 5), (0, 4),
+    (0, 6), (1, 5), (3, 0), (2, 5), (1, 4), (0, 7), (1, 6), (3, 1), (1, 7), (0, 8), (3, 3), (2, 6), (1, 8), (2, 7),
+    (3, 2), (2, 4), (3, 5), (0, 10), (0, 9), (2, 8), (1, 10), (3, 6), (1, 9), (3, 7), (3, 4), (4, 0), (5, 0),
+    (3, 8), (4, 1), (4, 3), (2, 10), (4, 2), (2, 9), (5, 1), (5, 3), (5, 2), (0, 11), (4, 5), (4, 4), (1, 11),
+    (3, 10), (4, 6), (5, 5), (3, 9), (0, 12), (4, 7), (5, 4), (5, 6), (1, 12), (5, 7), (4, 8), (0, 13), (0, 14),
+    (0, 15), (1, 13), (1, 14), (1, 15), (5, 8), (4, 10), (4, 9), (0, 17), (0, 16), (2, 11), (0, 18), (1, 17),
+    (3, 11), (5, 10), (1, 16), (1, 18), (2, 12), (5, 9), (3, 12), (0, 19), (0, 20), (2, 13), (1, 19), (1, 20),
+    (3, 13), (2, 14), (0, 21), (2, 15), (4, 11), (5, 11), (1, 21), (3, 14), (3, 15), (0, 22), (0, 23), (2, 17),
+    (2, 16), (3, 17), (4, 12), (1, 22), (1, 23), (2, 18), (3, 16), (5, 12), (2, 19), (2, 20), (3, 18), (4, 14),
+    (4, 13), (3, 19), (3, 20), (5, 13), (5, 14), (0, 24), (2, 21), (4, 18), (4, 17), (1, 24), (4, 15), (5, 15),
+    (4, 16), (3, 21), (5, 17), (2, 22), (2, 23), (4, 19), (4, 20), (5, 18), (3, 22), (3, 23), (5, 19), (5, 16),
+    (5, 20), (4, 21), (2, 24), (5, 21), (3, 24), (4, 22), (4, 23), (5, 22), (5, 23), (4, 24), (5, 24), (0, 25),
     (1, 25), (2, 25), (3, 25), (4, 25), (5, 25),
 )
 MESH = pl.DeviceIdType.MESH

time: 134 us -> 134 us (level)
  no operation moved by 1% of the time
where the time goes in v4:
time: 134 us; the launch traced here: 133 us
  Pallas kernels  107 us (80%)
  starting transfers between devices  11.1 us (8%)
  waiting for transfers between devices  6.2 us (5%)
  other arithmetic  3.72 us (3%)
  matrix products  2.58 us (2%)
  local copies, waits for them, and re-layouts  1.71 us (1%)
    pallas_call x1, Pallas kernels, two_hops(): pl.pallas_call(hops_kernel, out_shape=jax.ShapeDtypeStruct((PIECE, feat),...  96.9 us
    all_to_all x1, starting transfers between devices, local(): lax.all_to_all(outgoing.reshape(unit_count, per_pair, feature_width + CH)...  11.1 us
    pallas_call x1, Pallas kernels, build_block(): pl.pallas_call(block_kernel, grid_spec=pltpu.PrefetchScalarGridSpec(num_s...  10.1 us
    all_to_all x1, waiting for transfers between devices, local(): lax.all_to_all(outgoing.reshape(unit_count, per_pair, feature_width + CH)...  6.2 us
  transfers between devices with their start and end apart: 1, of which 1 were waited for; matrix products, arithmetic and copies ran while one was open for 0% of the time, Pallas kernels for 8%

profile of v4, /device:TPU:0, one launch (start us, length us, event | category | flops | bytes accessed | tf_op | source)
XLA Modules:
  0.0 133.2 jit_solution(865845549196772773)
XLA Ops:
  0.7 0.7 and_select_fusion.3
  1.4 0.2 convert_reduce_fusion
  1.6 0.1 broadcast_in_dim.17
  1.7 1.5 %convolution_convert_fusion = bf16[256,1664]{1,0:T(8,128)(2,1)S(1)} fusion(bf16[256,128]{1,0:T(8,128)(2,1)S(1)} %broadcast_in_dim.17, bf16[256,1536]{1,0:T(8,128)(2,1)} %param.7, s32[256]{0:T(256)S(1)} %add_select_fusion), kind=kOutput, calls=%fused_computation | convolution fusion | flops 220299264 | bytes 1704960 | tf_op jit(solution)/shard_map/dot_general | solution.py:427
  3.2 0.0 copy-start.1
  3.2 1.3 reshape.81
  4.5 11.1 %all-to-all-start = ((bf16[128,2,1664]{2,1,0:T(2,128)(2,1)}), bf16[128,2,1664]{2,1,0:T(2,128)(2,1)S(1)}, u32[]{:S(2)}, u32[]{:S(2)}) async-start(bf16[128,2,1664]{2,1,0:T(2,128)(2,1)} %reshape.81), calls=%async_computation | async-start | bytes 1703936 | tf_op jit(solution)/shard_map/all_to_all | solution.py:430
  15.7 0.0 copy-done.1
  15.7 0.6 select_reduce_fusion.slot_ref
  16.3 10.1 %build_block.1 = (bf16[2048,1024]{1,0:T(8,128)(2,1)}, bf16[1024,2048]{1,0:T(8,128)(2,1)}) custom-call(s32[128]{0:T(128)} %select_reduce_fusion.slot_ref, bf16[96,128,128]{2,1,0:T(8,128)(2,1)} %tiles_ref.1), custom_call_target="tpu_custom_call" | custom-call | bytes 25165824 | tf_op jit(solution)/shard_map/build_block/pallas_call | solution.py:65
  26.5 6.2 %all-to-all-done = bf16[128,2,1664]{2,1,0:T(2,128)(2,1)S(1)} async-done(((bf16[128,2,1664]{2,1,0:T(2,128)(2,1)}), bf16[128,2,1664]{2,1,0:T(2,128)(2,1)S(1)}, u32[]{:S(2)}, u32[]{:S(2)}) %all-to-all-start) | async-done | bytes 852000 | tf_op jit(solution)/shard_map/all_to_all | solution.py:430
  32.7 0.3 reshape.82
  33.0 0.1 add_reduce_fusion
  33.1 1.0 convolution_convert_fusion.1.features_ref
  34.1 0.0 copy-start
  34.1 96.9 %two_hops.1 = f32[128,1536]{1,0:T(8,128)} custom-call(bf16[128,1536]{1,0:T(8,128)(2,1)} %convolution_convert_fusion.1.features_ref, bf16[2048,1024]{1,0:T(8,128)(2,1)} %get-tuple-element.7.block_hbm, bf16[1024,2048]{1,0:T(8,128)(2,1)} %get-tuple-element.8.flipped_hbm, bf16[128,128]{1,0:T(8,128)(2,1)} %mix_in_ref.1, bf16[128,128]{1,0:T(8,128)(2,1)} %mix_out_ref.1), custom_call_target="tpu_custom_call" | custom-call | tf_op jit(solution)/shard_map/two_hops/pallas_call | solution.py:370
  131.1 0.0 copy-done
  131.1 2.1 %convert_subtract_fusion = f32[128,1536]{1,0:T(8,128)} fusion(f32[128,1536]{1,0:T(8,128)} %two_hops.1, bf16[128,1536]{1,0:T(8,128)(2,1)S(1)} %copy-done), kind=kLoop, calls=%fused_computation.6 | loop fusion | flops 393216 | bytes 1966080 | tf_op jit(solution)/shard_map/sub | solution.py:440
  (3 shorter events, 0.0 us)
Async XLA Ops:
  3.2 12.4 %copy-start.1 = (s32[96,2]{0,1:T(2,128)S(1)}, s32[96,2]{0,1:T(2,128)}, u32[]{:S(2)}) copy-start(s32[96,2]{0,1:T(2,128)} %param.10) | copy-start | bytes 2308
  4.5 28.1 %all-to-all-start = ((bf16[128,2,1664]{2,1,0:T(2,128)(2,1)}), bf16[128,2,1664]{2,1,0:T(2,128)(2,1)S(1)}, u32[]{:S(2)}, u32[]{:S(2)}) async-start(bf16[128,2,1664]{2,1,0:T(2,128)(2,1)} %reshape.81), calls=%async_computation | async-start | bytes 1703936 | tf_op jit(solution)/shard_map/all_to_all | solution.py:430
  34.1 96.9 %copy-start = (bf16[128,1536]{1,0:T(8,128)(2,1)S(1)}, bf16[128,1536]{1,0:T(8,128)(2,1)}, u32[]{:S(2)}) copy-start(bf16[128,1536]{1,0:T(8,128)(2,1)} %convolution_convert_fusion.1.features_ref) | copy-start | bytes 1179652
